TPU v7x, 512 devices: a whole 4x8x8 slice. The times are simulated.
512 devices in a mesh: ch: 128 (over y, z, core), grp: 4 (over x).
Axes of the slice: x: 4, y: 8, z: 8, core: 2. Of those that a mesh axis runs over, the one named last changes fastest.
Arguments:
- raw: bfloat16 [4, 1024, 2048], P('grp', 'ch'), may hold values from -400 to 400
- order: int32 [128, 16], P('ch'), may hold values from 0 to 15, each once within a row
- pair_blocks: int32 [128, 3], P('ch'), may hold values from -1 to 15, as said below
Outputs:
- corr: bfloat16 [2048, 3, 128, 256], P(('ch', 'grp'))
Inputs may be any that keep to these rules, and one draw needn't show every extreme that they name: `pair_blocks`: row i names distinct blocks among i * 16 // 128 - 1, i * 16 // 128, i * 16 // 128 + 1 that lie in 0 .. 15; slot 0 is always i * 16 // 128; live slots come first and empty ones hold -1.
All inputs are finite; a program needn't handle non-finite values.
Results may differ from a plain program's by a relative error of at most 0.013.
Values may be sent and summed in bfloat16 or wider, within the bound.
A program may use at most 128 MiB of HBM per device.

v0:
```python
import math
import jax
import jax.numpy as jnp
from jax import lax
from jax.sharding import PartitionSpec as P

SRC = 128
SEG = 256
LAGS = 256
SMOOTH = 8
MAXP = 3
REACH = 15
lag_scale = 1.0 / 16.0


def from_behind(value, axis, steps):
    count = lax.axis_size(axis)
    initial, last = (max(0, -steps), min(count, count - steps))
    return lax.ppermute(value, axis, [(source, source + steps) for source in range(initial, last)])


def transform_tables(half_len, lag_count, smooth_half):
    samples = jnp.arange(half_len, dtype=jnp.int32)
    column = jnp.arange(2 * half_len, dtype=jnp.int32)
    freq = column % half_len + 1
    phase_fwd = samples[:, None] * freq[None, :] % (2 * half_len)
    angle_fwd = phase_fwd.astype(jnp.float32) * (math.pi / half_len)
    forward = jnp.where(column[None, :] < half_len, jnp.cos(angle_fwd), -jnp.sin(angle_fwd)).astype(
        jnp.bfloat16
    )
    lag_steps = jnp.arange(lag_count, dtype=jnp.int32) - lag_count // 2
    phase_inv = freq[:, None] * lag_steps[None, :] % (2 * half_len)
    angle_inv = phase_inv.astype(jnp.float32) * (math.pi / half_len)
    inverse = (
        jnp.where(column[:, None] < half_len, jnp.cos(angle_inv), -jnp.sin(angle_inv)) * lag_scale
    ).astype(jnp.bfloat16)
    bins = jnp.arange(half_len, dtype=jnp.int32)
    smoothing = (jnp.abs(bins[:, None] - bins[None, :]) <= smooth_half).astype(jnp.float32) / (
        2 * smooth_half + 1
    )
    return (forward, inverse, smoothing)


def whiten(segments, forward, smoothing):
    half_len = segments.shape[-1]
    flat_rows = segments.reshape(-1, half_len)
    spectrum = jnp.dot(flat_rows, forward, preferred_element_type=jnp.float32)
    real_part = spectrum[:, :half_len]
    imag_part = spectrum[:, half_len:]
    power_bins = real_part * real_part + imag_part * imag_part
    smoothed = jnp.dot(power_bins, smoothing, precision=lax.Precision.HIGHEST)
    water_level = jnp.mean(power_bins, axis=1, keepdims=True)
    divisor = jnp.sqrt(smoothed + 0.1 * water_level + 1e-06)
    whitened = spectrum / jnp.concatenate([divisor, divisor], axis=1)
    return whitened.astype(jnp.bfloat16).reshape(segments.shape[:-1] + (2 * half_len,))


def correlate(receivers, sources, inverse):
    half_len = receivers.shape[-1] // 2
    seg_count = receivers.shape[1]
    recv_re = receivers[..., :half_len]
    recv_im = receivers[..., half_len:]
    left_first = jnp.concatenate([recv_re, recv_im], axis=1)
    left_second = jnp.concatenate([recv_im, -recv_re], axis=1)
    right_both = jnp.concatenate([sources[..., :half_len], sources[..., half_len:]], axis=1)
    cross_re = jnp.einsum(
        "rnk,snk->rsk", left_first, right_both, preferred_element_type=jnp.float32
    )
    cross_im = jnp.einsum(
        "rnk,snk->rsk", left_second, right_both, preferred_element_type=jnp.float32
    )
    cross_spec = (jnp.concatenate([cross_re, cross_im], axis=2) * (1.0 / seg_count)).astype(
        jnp.bfloat16
    )
    recv_count = receivers.shape[0]
    src_count = sources.shape[0]
    lag_values = jnp.dot(
        cross_spec.reshape(-1, 2 * half_len), inverse, preferred_element_type=jnp.float32
    )
    return lag_values.reshape(recv_count, src_count, inverse.shape[1])


def local(raw, order, pair_blocks):
    recorded = lax.all_to_all(raw, "ch", split_axis=2, concat_axis=1, tiled=True)
    local_channels = recorded.shape[2]
    onehot = (order[0][:, None] == jnp.arange(local_channels, dtype=jnp.int32)[None, :]).astype(
        jnp.bfloat16
    )
    series = jnp.einsum(
        "ck,tc->kt", onehot, recorded[0], preferred_element_type=jnp.float32
    ).astype(jnp.bfloat16)
    segments = series.reshape(1, local_channels, -1, SEG)
    forward, inverse, smoothing = transform_tables(SEG, LAGS, SMOOTH)
    own_white = whiten(segments, forward, smoothing)
    before_list = []
    for distance in range(REACH, 0, -1):
        before_list.append(from_behind(own_white, "ch", distance))
    after_list = []
    for distance in range(1, REACH + 1):
        after_list.append(from_behind(own_white, "ch", -distance))
    window = jnp.concatenate(before_list + [own_white] + after_list, axis=1)
    window_base = (lax.axis_index("ch") - REACH) * local_channels
    groups = lax.axis_size("grp")
    receivers = own_white[0]
    slot_results = []
    for slot_index in range(MAXP):
        block_id = pair_blocks[0, slot_index]
        source_start = jnp.maximum(block_id, 0) * SRC - window_base
        sources = lax.dynamic_slice_in_dim(window[0], source_start, SRC, 0)
        is_live = (block_id >= 0).astype(jnp.float32)
        lag_values = correlate(receivers, sources, inverse) * is_live
        slot_results.append(lag_values)
    stacked = lax.psum_scatter(
        jnp.stack(slot_results, axis=1).astype(jnp.bfloat16), "grp", scatter_dimension=0, tiled=True
    ).astype(jnp.float32)
    return (stacked / groups).astype(jnp.bfloat16)


def solution(mesh):
    placed = (P("grp", "ch", None), P("ch", None), P("ch", None))
    return jax.shard_map(
        local,
        mesh=mesh,
        in_specs=placed,
        out_specs=P(("ch", "grp"), None, None, None),
        check_vma=False,
    )
```

profile of v0, /device:TPU:1, one launch (start us, length us, event | category | flops | bytes accessed | tf_op | source)
XLA Modules:
  0.0 307.8 jit_solution(12834081129532482578)
XLA Ops:
  6.5 3.1 %copy.19 = bf16[1,8,2048]{1,0,2:T(2,128)(2,1)} copy(bf16[1,8,2048]{2,1,0:T(8,128)(2,1)} %param.3) | data formatting | bytes 65536 | tf_op args[0]
  9.7 18.5 %all-to-all-start = ((bf16[1,8,2048]{1,0,2:T(2,128)(2,1)}), bf16[1,8,2048]{1,0,2:T(2,128)(2,1)S(1)}, u32[]{:S(2)}, u32[]{:S(2)}) async-start(bf16[1,8,2048]{1,0,2:T(2,128)(2,1)} %copy.19), calls=%async_computation | async-start | bytes 2097152 | tf_op jit(solution)/shard_map/all_to_all | solution.py:84
  28.3 0.6 fusion.99
  32.8 25.9 %all-to-all-done = bf16[1,8,2048]{1,0,2:T(2,128)(2,1)S(1)} async-done(((bf16[1,8,2048]{1,0,2:T(2,128)(2,1)}), bf16[1,8,2048]{1,0,2:T(2,128)(2,1)S(1)}, u32[]{:S(2)}, u32[]{:S(2)}) %all-to-all-start) | async-done | bytes 32800 | tf_op jit(solution)/shard_map/all_to_all | solution.py:84
  59.7 2.4 fusion.48
  62.6 4.5 %collective-permute-start = (bf16[1,16,4,512]{3,2,1,0:T(4,128)(2,1)S(1)}, bf16[1,16,4,512]{3,2,1,0:T(4,128)(2,1)S(1)}, u32[]{:S(2)}, u32[]{:S(2)}) collective-permute-start(bf16[1,16,4,512]{3,2,1,0:T(4,128)(2,1)S(1)} %reshape.97), channel_id=1, source_target_pairs={{0,60},{4,64},{8,68},{12,72},{16,76},{20,80},{24,84},{28,88},{32,9... | collective-permute-start | bytes 196616 | tf_op jit(solution)/shard_map/ppermute | solution.py:19
  67.1 1.4 collective-permute-start.1
  68.4 3.3 %collective-permute-start.2 = (bf16[1,16,4,512]{3,2,1,0:T(4,128)(2,1)S(1)}, bf16[1,16,4,512]{3,2,1,0:T(4,128)(2,1)S(1)}, u32[]{:S(2)}, u32[]{:S(2)}) collective-permute-start(bf16[1,16,4,512]{3,2,1,0:T(4,128)(2,1)S(1)} %reshape.97), channel_id=1, source_target_pairs={{0,52},{4,56},{8,60},{12,64},{16,68},{20,72},{24,76},{28,80},{32,8... | collective-permute-start | bytes 196616 | tf_op jit(solution)/shard_map/ppermute | solution.py:19
  71.7 4.7 %collective-permute-start.3 = (bf16[1,16,4,512]{3,2,1,0:T(4,128)(2,1)S(1)}, bf16[1,16,4,512]{3,2,1,0:T(4,128)(2,1)S(1)}, u32[]{:S(2)}, u32[]{:S(2)}) collective-permute-start(bf16[1,16,4,512]{3,2,1,0:T(4,128)(2,1)S(1)} %reshape.97), channel_id=1, source_target_pairs={{0,48},{4,52},{8,56},{12,60},{16,64},{20,68},{24,72},{28,76},{32,8... | collective-permute-start | bytes 196616 | tf_op jit(solution)/shard_map/ppermute | solution.py:19
  76.5 4.3 %collective-permute-start.4 = (bf16[1,16,4,512]{3,2,1,0:T(4,128)(2,1)S(1)}, bf16[1,16,4,512]{3,2,1,0:T(4,128)(2,1)S(1)}, u32[]{:S(2)}, u32[]{:S(2)}) collective-permute-start(bf16[1,16,4,512]{3,2,1,0:T(4,128)(2,1)S(1)} %reshape.97), channel_id=1, source_target_pairs={{0,44},{4,48},{8,52},{12,56},{16,60},{20,64},{24,68},{28,72},{32,7... | collective-permute-start | bytes 196616 | tf_op jit(solution)/shard_map/ppermute | solution.py:19
  81.6 3.6 %collective-permute-start.5 = (bf16[1,16,4,512]{3,2,1,0:T(4,128)(2,1)S(1)}, bf16[1,16,4,512]{3,2,1,0:T(4,128)(2,1)S(1)}, u32[]{:S(2)}, u32[]{:S(2)}) collective-permute-start(bf16[1,16,4,512]{3,2,1,0:T(4,128)(2,1)S(1)} %reshape.97), channel_id=1, source_target_pairs={{0,40},{4,44},{8,48},{12,52},{16,56},{20,60},{24,64},{28,68},{32,7... | collective-permute-start | bytes 196616 | tf_op jit(solution)/shard_map/ppermute | solution.py:19
  85.3 5.7 %collective-permute-start.6 = (bf16[1,16,4,512]{3,2,1,0:T(4,128)(2,1)S(1)}, bf16[1,16,4,512]{3,2,1,0:T(4,128)(2,1)S(1)}, u32[]{:S(2)}, u32[]{:S(2)}) collective-permute-start(bf16[1,16,4,512]{3,2,1,0:T(4,128)(2,1)S(1)} %reshape.97), channel_id=1, source_target_pairs={{0,36},{4,40},{8,44},{12,48},{16,52},{20,56},{24,60},{28,64},{32,6... | collective-permute-start | bytes 196616 | tf_op jit(solution)/shard_map/ppermute | solution.py:19
  91.1 3.6 %collective-permute-start.7 = (bf16[1,16,4,512]{3,2,1,0:T(4,128)(2,1)S(1)}, bf16[1,16,4,512]{3,2,1,0:T(4,128)(2,1)S(1)}, u32[]{:S(2)}, u32[]{:S(2)}) collective-permute-start(bf16[1,16,4,512]{3,2,1,0:T(4,128)(2,1)S(1)} %reshape.97), channel_id=1, source_target_pairs={{0,32},{4,36},{8,40},{12,44},{16,48},{20,52},{24,56},{28,60},{32,6... | collective-permute-start | bytes 196616 | tf_op jit(solution)/shard_map/ppermute | solution.py:19
  94.8 7.2 %collective-permute-start.8 = (bf16[1,16,4,512]{3,2,1,0:T(4,128)(2,1)S(1)}, bf16[1,16,4,512]{3,2,1,0:T(4,128)(2,1)S(1)}, u32[]{:S(2)}, u32[]{:S(2)}) collective-permute-start(bf16[1,16,4,512]{3,2,1,0:T(4,128)(2,1)S(1)} %reshape.97), channel_id=1, source_target_pairs={{0,28},{4,32},{8,36},{12,40},{16,44},{20,48},{24,52},{28,56},{32,6... | collective-permute-start | bytes 196616 | tf_op jit(solution)/shard_map/ppermute | solution.py:19
  102.0 1.3 collective-permute-start.9
  103.3 4.9 %collective-permute-start.10 = (bf16[1,16,4,512]{3,2,1,0:T(4,128)(2,1)S(1)}, bf16[1,16,4,512]{3,2,1,0:T(4,128)(2,1)S(1)}, u32[]{:S(2)}, u32[]{:S(2)}) collective-permute-start(bf16[1,16,4,512]{3,2,1,0:T(4,128)(2,1)S(1)} %reshape.97), channel_id=1, source_target_pairs={{0,20},{4,24},{8,28},{12,32},{16,36},{20,40},{24,44},{28,48},{32,5... | collective-permute-start | bytes 196616 | tf_op jit(solution)/shard_map/ppermute | solution.py:19
  108.3 4.0 %collective-permute-start.11 = (bf16[1,16,4,512]{3,2,1,0:T(4,128)(2,1)S(1)}, bf16[1,16,4,512]{3,2,1,0:T(4,128)(2,1)S(1)}, u32[]{:S(2)}, u32[]{:S(2)}) collective-permute-start(bf16[1,16,4,512]{3,2,1,0:T(4,128)(2,1)S(1)} %reshape.97), channel_id=1, source_target_pairs={{0,16},{4,20},{8,24},{12,28},{16,32},{20,36},{24,40},{28,44},{32,4... | collective-permute-start | bytes 196616 | tf_op jit(solution)/shard_map/ppermute | solution.py:19
  112.4 5.1 %collective-permute-start.12 = (bf16[1,16,4,512]{3,2,1,0:T(4,128)(2,1)S(1)}, bf16[1,16,4,512]{3,2,1,0:T(4,128)(2,1)S(1)}, u32[]{:S(2)}, u32[]{:S(2)}) collective-permute-start(bf16[1,16,4,512]{3,2,1,0:T(4,128)(2,1)S(1)} %reshape.97), channel_id=1, source_target_pairs={{0,12},{4,16},{8,20},{12,24},{16,28},{20,32},{24,36},{28,40},{32,4... | collective-permute-start | bytes 196616 | tf_op jit(solution)/shard_map/ppermute | solution.py:19
  117.5 1.7 collective-permute-start.13
  119.3 2.7 collective-permute-start.14
  122.0 1.9 collective-permute-start.15
  124.0 1.3 collective-permute-start.16
  125.3 1.3 collective-permute-start.17
  126.7 1.3 collective-permute-start.18
  128.0 1.3 collective-permute-start.19
  129.4 1.3 collective-permute-start.20
  130.8 1.3 collective-permute-start.21
  132.1 1.5 collective-permute-done.17
  133.6 1.3 collective-permute-start.22
  134.9 0.7 collective-permute-done.18
  135.6 1.3 collective-permute-start.23
  136.9 2.9 collective-permute-done.19
  139.8 1.3 collective-permute-start.24
  141.1 2.4 collective-permute-done.20
  143.5 1.3 collective-permute-start.25
  144.8 1.3 collective-permute-start.26
  146.3 1.3 collective-permute-start.27
  147.6 1.1 collective-permute-done.23
  148.7 1.3 collective-permute-start.28
  150.0 1.4 collective-permute-done.24
  151.4 1.3 collective-permute-start.29
  152.7 4.3 %collective-permute-done.25 = bf16[1,16,4,512]{3,2,1,0:T(4,128)(2,1)S(1)} collective-permute-done((bf16[1,16,4,512]{3,2,1,0:T(4,128)(2,1)S(1)}, bf16[1,16,4,512]{3,2,1,0:T(4,128)(2,1)S(1)}, u32[]{:S(2)}, u32[]{:S(2)}) %collective-permute-start.25) | collective-permute-done | bytes 65568 | tf_op jit(solution)/shard_map/ppermute | solution.py:19
  157.0 2.7 collective-permute-done.26
  159.7 8.3 %collective-permute-done.27 = bf16[1,16,4,512]{3,2,1,0:T(4,128)(2,1)S(1)} collective-permute-done((bf16[1,16,4,512]{3,2,1,0:T(4,128)(2,1)S(1)}, bf16[1,16,4,512]{3,2,1,0:T(4,128)(2,1)S(1)}, u32[]{:S(2)}, u32[]{:S(2)}) %collective-permute-start.27) | collective-permute-done | bytes 65568 | tf_op jit(solution)/shard_map/ppermute | solution.py:19
  168.6 2.2 collective-permute-done.29
  170.7 1.5 constant_dynamic-slice_fusion.2
  173.6 1.9 convolution_bitcast_fusion.4
  175.6 2.1 copy.26
  177.7 1.2 fusion.96
  178.9 2.0 convolution_bitcast_fusion.3
  180.9 1.9 convolution_bitcast_fusion.2
  182.8 2.2 copy.30
  185.0 1.2 fusion.97
  187.4 1.0 copy-done
  188.8 1.2 copy-done.1
  190.0 0.6 copy-done.2
  191.0 3.4 %fusion.15 = bf16[16,1,128,256]{3,2,0,1:T(8,128)(2,1)S(1)} fusion(bf16[16,128,512]{1,0,2:T(8,128)(2,1)S(1)} %fusion, f32[]{:T(128)} %bitcast.8, s32[256]{0:T(256)S(1)} %iota_add_fusion, s32[512]{0:T(512)S(1)} %fusion.63, pred[512]{0:T(512)(128)(4,1)S(1)} %iota_compare_fusion.1), kind=kOutput, calls=%fused_computation.23 | convolution fusion | flops 540278784 | bytes 3149316 | tf_op jit(solution)/shard_map/dot_general | solution.py:77
  194.4 3.4 %fusion.18 = bf16[16,1,128,256]{3,2,0,1:T(8,128)(2,1)S(1)} fusion(bf16[16,128,512]{1,0,2:T(8,128)(2,1)S(1)} %fusion.1, f32[]{:T(128)} %bitcast.14, s32[256]{0:T(256)S(1)} %iota_add_fusion, s32[512]{0:T(512)S(1)} %fusion.63, pred[512]{0:T(512)(128)(4,1)S(1)} %iota_compare_fusion.1), kind=kOutput, calls=%fused_computation.24 | convolution fusion | flops 540278784 | bytes 3149316 | tf_op jit(solution)/shard_map/dot_general | solution.py:77
  198.1 3.4 %fusion.21 = bf16[16,1,128,256]{3,2,0,1:T(8,128)(2,1)S(1)} fusion(bf16[16,128,512]{1,0,2:T(8,128)(2,1)S(1)} %fusion.2, f32[]{:T(128)} %bitcast.20, s32[256]{0:T(256)S(1)} %iota_add_fusion, s32[512]{0:T(512)S(1)} %fusion.63, pred[512]{0:T(512)(128)(4,1)S(1)} %iota_compare_fusion.1), kind=kOutput, calls=%fused_computation.25 | convolution fusion | flops 540278784 | bytes 3149316 | tf_op jit(solution)/shard_map/dot_general | solution.py:77
  201.5 2.0 pad_maximum_fusion
  203.6 1.3 dynamic-slice.3
  205.5 93.2 %all-reduce.3.cloned.1.call-done = bf16[16,3,128,256]{3,2,0,1:T(8,128)(2,1)} async-done(((bf16[16,3,128,256]{3,2,0,1:T(8,128)(2,1)}), bf16[16,3,128,256]{3,2,0,1:T(8,128)(2,1)}) %all-reduce.3.cloned.1.call-update) | async-done | bytes 3145744
  298.7 1.3 multiply_convert_fusion.3
  300.0 0.9 copy.34
  (85 shorter events, 7.6 us)
Async XLA Ops:
  6.5 21.8 %copy-start.3 = (s32[1,3]{1,0:T(1,128)S(1)}, s32[1,3]{1,0:T(1,128)}, u32[]{:S(2)}) copy-start(s32[1,3]{1,0:T(1,128)} %param.5) | copy-start | bytes 40
  9.7 49.7 %copy-start.4 = (s32[1,16]{1,0:T(1,128)S(1)}, s32[1,16]{1,0:T(1,128)}, u32[]{:S(2)}) copy-start(s32[1,16]{1,0:T(1,128)} %param.4) | copy-start | bytes 196
  9.7 49.0 %all-to-all-start = ((bf16[1,8,2048]{1,0,2:T(2,128)(2,1)}), bf16[1,8,2048]{1,0,2:T(2,128)(2,1)S(1)}, u32[]{:S(2)}, u32[]{:S(2)}) async-start(bf16[1,8,2048]{1,0,2:T(2,128)(2,1)} %copy.19), calls=%async_computation | async-start | bytes 2097152 | tf_op jit(solution)/shard_map/all_to_all | solution.py:84
  28.2 270.5 %all-reduce.3.cloned.1.call-start = ((), (), s32[]{:S(2)}) async-start(), calls=%async_computation.1 | async-start | bytes 6291456
  62.6 19.0 %collective-permute-start = (bf16[1,16,4,512]{3,2,1,0:T(4,128)(2,1)S(1)}, bf16[1,16,4,512]{3,2,1,0:T(4,128)(2,1)S(1)}, u32[]{:S(2)}, u32[]{:S(2)}) collective-permute-start(bf16[1,16,4,512]{3,2,1,0:T(4,128)(2,1)S(1)} %reshape.97), channel_id=1, source_target_pairs={{0,60},{4,64},{8,68},{12,72},{16,76},{20,80},{24,84},{28,88},{32,9... | collective-permute-start | bytes 196616 | tf_op jit(solution)/shard_map/ppermute | solution.py:19
  67.1 18.2 %collective-permute-start.1 = (bf16[1,16,4,512]{3,2,1,0:T(4,128)(2,1)S(1)}, bf16[1,16,4,512]{3,2,1,0:T(4,128)(2,1)S(1)}, u32[]{:S(2)}, u32[]{:S(2)}) collective-permute-start(bf16[1,16,4,512]{3,2,1,0:T(4,128)(2,1)S(1)} %reshape.97), channel_id=1, source_target_pairs={{0,56},{4,60},{8,64},{12,68},{16,72},{20,76},{24,80},{28,84},{32,8... | collective-permute-start | bytes 196616 | tf_op jit(solution)/shard_map/ppermute | solution.py:19
  68.4 22.7 %collective-permute-start.2 = (bf16[1,16,4,512]{3,2,1,0:T(4,128)(2,1)S(1)}, bf16[1,16,4,512]{3,2,1,0:T(4,128)(2,1)S(1)}, u32[]{:S(2)}, u32[]{:S(2)}) collective-permute-start(bf16[1,16,4,512]{3,2,1,0:T(4,128)(2,1)S(1)} %reshape.97), channel_id=1, source_target_pairs={{0,52},{4,56},{8,60},{12,64},{16,68},{20,72},{24,76},{28,80},{32,8... | collective-permute-start | bytes 196616 | tf_op jit(solution)/shard_map/ppermute | solution.py:19
  71.7 23.0 %collective-permute-start.3 = (bf16[1,16,4,512]{3,2,1,0:T(4,128)(2,1)S(1)}, bf16[1,16,4,512]{3,2,1,0:T(4,128)(2,1)S(1)}, u32[]{:S(2)}, u32[]{:S(2)}) collective-permute-start(bf16[1,16,4,512]{3,2,1,0:T(4,128)(2,1)S(1)} %reshape.97), channel_id=1, source_target_pairs={{0,48},{4,52},{8,56},{12,60},{16,64},{20,68},{24,72},{28,76},{32,8... | collective-permute-start | bytes 196616 | tf_op jit(solution)/shard_map/ppermute | solution.py:19
  76.5 25.5 %collective-permute-start.4 = (bf16[1,16,4,512]{3,2,1,0:T(4,128)(2,1)S(1)}, bf16[1,16,4,512]{3,2,1,0:T(4,128)(2,1)S(1)}, u32[]{:S(2)}, u32[]{:S(2)}) collective-permute-start(bf16[1,16,4,512]{3,2,1,0:T(4,128)(2,1)S(1)} %reshape.97), channel_id=1, source_target_pairs={{0,44},{4,48},{8,52},{12,56},{16,60},{20,64},{24,68},{28,72},{32,7... | collective-permute-start | bytes 196616 | tf_op jit(solution)/shard_map/ppermute | solution.py:19
  81.6 21.7 %collective-permute-start.5 = (bf16[1,16,4,512]{3,2,1,0:T(4,128)(2,1)S(1)}, bf16[1,16,4,512]{3,2,1,0:T(4,128)(2,1)S(1)}, u32[]{:S(2)}, u32[]{:S(2)}) collective-permute-start(bf16[1,16,4,512]{3,2,1,0:T(4,128)(2,1)S(1)} %reshape.97), channel_id=1, source_target_pairs={{0,40},{4,44},{8,48},{12,52},{16,56},{20,60},{24,64},{28,68},{32,7... | collective-permute-start | bytes 196616 | tf_op jit(solution)/shard_map/ppermute | solution.py:19
  85.3 23.0 %collective-permute-start.6 = (bf16[1,16,4,512]{3,2,1,0:T(4,128)(2,1)S(1)}, bf16[1,16,4,512]{3,2,1,0:T(4,128)(2,1)S(1)}, u32[]{:S(2)}, u32[]{:S(2)}) collective-permute-start(bf16[1,16,4,512]{3,2,1,0:T(4,128)(2,1)S(1)} %reshape.97), channel_id=1, source_target_pairs={{0,36},{4,40},{8,44},{12,48},{16,52},{20,56},{24,60},{28,64},{32,6... | collective-permute-start | bytes 196616 | tf_op jit(solution)/shard_map/ppermute | solution.py:19
  91.1 21.3 %collective-permute-start.7 = (bf16[1,16,4,512]{3,2,1,0:T(4,128)(2,1)S(1)}, bf16[1,16,4,512]{3,2,1,0:T(4,128)(2,1)S(1)}, u32[]{:S(2)}, u32[]{:S(2)}) collective-permute-start(bf16[1,16,4,512]{3,2,1,0:T(4,128)(2,1)S(1)} %reshape.97), channel_id=1, source_target_pairs={{0,32},{4,36},{8,40},{12,44},{16,48},{20,52},{24,56},{28,60},{32,6... | collective-permute-start | bytes 196616 | tf_op jit(solution)/shard_map/ppermute | solution.py:19
  94.8 22.7 %collective-permute-start.8 = (bf16[1,16,4,512]{3,2,1,0:T(4,128)(2,1)S(1)}, bf16[1,16,4,512]{3,2,1,0:T(4,128)(2,1)S(1)}, u32[]{:S(2)}, u32[]{:S(2)}) collective-permute-start(bf16[1,16,4,512]{3,2,1,0:T(4,128)(2,1)S(1)} %reshape.97), channel_id=1, source_target_pairs={{0,28},{4,32},{8,36},{12,40},{16,44},{20,48},{24,52},{28,56},{32,6... | collective-permute-start | bytes 196616 | tf_op jit(solution)/shard_map/ppermute | solution.py:19
  102.0 17.3 %collective-permute-start.9 = (bf16[1,16,4,512]{3,2,1,0:T(4,128)(2,1)S(1)}, bf16[1,16,4,512]{3,2,1,0:T(4,128)(2,1)S(1)}, u32[]{:S(2)}, u32[]{:S(2)}) collective-permute-start(bf16[1,16,4,512]{3,2,1,0:T(4,128)(2,1)S(1)} %reshape.97), channel_id=1, source_target_pairs={{0,24},{4,28},{8,32},{12,36},{16,40},{20,44},{24,48},{28,52},{32,5... | collective-permute-start | bytes 196616 | tf_op jit(solution)/shard_map/ppermute | solution.py:19
  103.3 18.7 %collective-permute-start.10 = (bf16[1,16,4,512]{3,2,1,0:T(4,128)(2,1)S(1)}, bf16[1,16,4,512]{3,2,1,0:T(4,128)(2,1)S(1)}, u32[]{:S(2)}, u32[]{:S(2)}) collective-permute-start(bf16[1,16,4,512]{3,2,1,0:T(4,128)(2,1)S(1)} %reshape.97), channel_id=1, source_target_pairs={{0,20},{4,24},{8,28},{12,32},{16,36},{20,40},{24,44},{28,48},{32,5... | collective-permute-start | bytes 196616 | tf_op jit(solution)/shard_map/ppermute | solution.py:19
  108.3 15.6 %collective-permute-start.11 = (bf16[1,16,4,512]{3,2,1,0:T(4,128)(2,1)S(1)}, bf16[1,16,4,512]{3,2,1,0:T(4,128)(2,1)S(1)}, u32[]{:S(2)}, u32[]{:S(2)}) collective-permute-start(bf16[1,16,4,512]{3,2,1,0:T(4,128)(2,1)S(1)} %reshape.97), channel_id=1, source_target_pairs={{0,16},{4,20},{8,24},{12,28},{16,32},{20,36},{24,40},{28,44},{32,4... | collective-permute-start | bytes 196616 | tf_op jit(solution)/shard_map/ppermute | solution.py:19
  112.4 12.9 %collective-permute-start.12 = (bf16[1,16,4,512]{3,2,1,0:T(4,128)(2,1)S(1)}, bf16[1,16,4,512]{3,2,1,0:T(4,128)(2,1)S(1)}, u32[]{:S(2)}, u32[]{:S(2)}) collective-permute-start(bf16[1,16,4,512]{3,2,1,0:T(4,128)(2,1)S(1)} %reshape.97), channel_id=1, source_target_pairs={{0,12},{4,16},{8,20},{12,24},{16,28},{20,32},{24,36},{28,40},{32,4... | collective-permute-start | bytes 196616 | tf_op jit(solution)/shard_map/ppermute | solution.py:19
  117.5 9.2 %collective-permute-start.13 = (bf16[1,16,4,512]{3,2,1,0:T(4,128)(2,1)S(1)}, bf16[1,16,4,512]{3,2,1,0:T(4,128)(2,1)S(1)}, u32[]{:S(2)}, u32[]{:S(2)}) collective-permute-start(bf16[1,16,4,512]{3,2,1,0:T(4,128)(2,1)S(1)} %reshape.97), channel_id=1, source_target_pairs={{0,8},{4,12},{8,16},{12,20},{16,24},{20,28},{24,32},{28,36},{32,40... | collective-permute-start | bytes 196616 | tf_op jit(solution)/shard_map/ppermute | solution.py:19
  119.3 8.8 %collective-permute-start.14 = (bf16[1,16,4,512]{3,2,1,0:T(4,128)(2,1)S(1)}, bf16[1,16,4,512]{3,2,1,0:T(4,128)(2,1)S(1)}, u32[]{:S(2)}, u32[]{:S(2)}) collective-permute-start(bf16[1,16,4,512]{3,2,1,0:T(4,128)(2,1)S(1)} %reshape.97), channel_id=1, source_target_pairs={{0,4},{4,8},{8,12},{12,16},{16,20},{20,24},{24,28},{28,32},{32,36}... | collective-permute-start | bytes 196616 | tf_op jit(solution)/shard_map/ppermute | solution.py:19
  122.0 7.4 %collective-permute-start.15 = (bf16[1,16,4,512]{3,2,1,0:T(4,128)(2,1)S(1)}, bf16[1,16,4,512]{3,2,1,0:T(4,128)(2,1)S(1)}, u32[]{:S(2)}, u32[]{:S(2)}) collective-permute-start(bf16[1,16,4,512]{3,2,1,0:T(4,128)(2,1)S(1)} %reshape.97), channel_id=1, source_target_pairs={{4,0},{8,4},{12,8},{16,12},{20,16},{24,20},{28,24},{32,28},{36,32}... | collective-permute-start | bytes 196616 | tf_op jit(solution)/shard_map/ppermute | solution.py:19
  124.0 6.8 %collective-permute-start.16 = (bf16[1,16,4,512]{3,2,1,0:T(4,128)(2,1)S(1)}, bf16[1,16,4,512]{3,2,1,0:T(4,128)(2,1)S(1)}, u32[]{:S(2)}, u32[]{:S(2)}) collective-permute-start(bf16[1,16,4,512]{3,2,1,0:T(4,128)(2,1)S(1)} %reshape.97), channel_id=1, source_target_pairs={{8,0},{12,4},{16,8},{20,12},{24,16},{28,20},{32,24},{36,28},{40,32... | collective-permute-start | bytes 196616 | tf_op jit(solution)/shard_map/ppermute | solution.py:19
  125.3 8.3 %collective-permute-start.17 = (bf16[1,16,4,512]{3,2,1,0:T(4,128)(2,1)S(1)}, bf16[1,16,4,512]{3,2,1,0:T(4,128)(2,1)S(1)}, u32[]{:S(2)}, u32[]{:S(2)}) collective-permute-start(bf16[1,16,4,512]{3,2,1,0:T(4,128)(2,1)S(1)} %reshape.97), channel_id=1, source_target_pairs={{12,0},{16,4},{20,8},{24,12},{28,16},{32,20},{36,24},{40,28},{44,3... | collective-permute-start | bytes 196616 | tf_op jit(solution)/shard_map/ppermute | solution.py:19
  126.7 8.9 %collective-permute-start.18 = (bf16[1,16,4,512]{3,2,1,0:T(4,128)(2,1)S(1)}, bf16[1,16,4,512]{3,2,1,0:T(4,128)(2,1)S(1)}, u32[]{:S(2)}, u32[]{:S(2)}) collective-permute-start(bf16[1,16,4,512]{3,2,1,0:T(4,128)(2,1)S(1)} %reshape.97), channel_id=1, source_target_pairs={{16,0},{20,4},{24,8},{28,12},{32,16},{36,20},{40,24},{44,28},{48,3... | collective-permute-start | bytes 196616 | tf_op jit(solution)/shard_map/ppermute | solution.py:19
  128.0 11.7 %collective-permute-start.19 = (bf16[1,16,4,512]{3,2,1,0:T(4,128)(2,1)S(1)}, bf16[1,16,4,512]{3,2,1,0:T(4,128)(2,1)S(1)}, u32[]{:S(2)}, u32[]{:S(2)}) collective-permute-start(bf16[1,16,4,512]{3,2,1,0:T(4,128)(2,1)S(1)} %reshape.97), channel_id=1, source_target_pairs={{20,0},{24,4},{28,8},{32,12},{36,16},{40,20},{44,24},{48,28},{52,3... | collective-permute-start | bytes 196616 | tf_op jit(solution)/shard_map/ppermute | solution.py:19
  129.4 14.1 %collective-permute-start.20 = (bf16[1,16,4,512]{3,2,1,0:T(4,128)(2,1)S(1)}, bf16[1,16,4,512]{3,2,1,0:T(4,128)(2,1)S(1)}, u32[]{:S(2)}, u32[]{:S(2)}) collective-permute-start(bf16[1,16,4,512]{3,2,1,0:T(4,128)(2,1)S(1)} %reshape.97), channel_id=1, source_target_pairs={{24,0},{28,4},{32,8},{36,12},{40,16},{44,20},{48,24},{52,28},{56,3... | collective-permute-start | bytes 196616 | tf_op jit(solution)/shard_map/ppermute | solution.py:19
  130.8 14.1 %collective-permute-start.21 = (bf16[1,16,4,512]{3,2,1,0:T(4,128)(2,1)S(1)}, bf16[1,16,4,512]{3,2,1,0:T(4,128)(2,1)S(1)}, u32[]{:S(2)}, u32[]{:S(2)}) collective-permute-start(bf16[1,16,4,512]{3,2,1,0:T(4,128)(2,1)S(1)} %reshape.97), channel_id=1, source_target_pairs={{28,0},{32,4},{36,8},{40,12},{44,16},{48,20},{52,24},{56,28},{60,3... | collective-permute-start | bytes 196616 | tf_op jit(solution)/shard_map/ppermute | solution.py:19
  133.6 12.7 %collective-permute-start.22 = (bf16[1,16,4,512]{3,2,1,0:T(4,128)(2,1)S(1)}, bf16[1,16,4,512]{3,2,1,0:T(4,128)(2,1)S(1)}, u32[]{:S(2)}, u32[]{:S(2)}) collective-permute-start(bf16[1,16,4,512]{3,2,1,0:T(4,128)(2,1)S(1)} %reshape.97), channel_id=1, source_target_pairs={{32,0},{36,4},{40,8},{44,12},{48,16},{52,20},{56,24},{60,28},{64,3... | collective-permute-start | bytes 196616 | tf_op jit(solution)/shard_map/ppermute | solution.py:19
  135.6 13.1 %collective-permute-start.23 = (bf16[1,16,4,512]{3,2,1,0:T(4,128)(2,1)S(1)}, bf16[1,16,4,512]{3,2,1,0:T(4,128)(2,1)S(1)}, u32[]{:S(2)}, u32[]{:S(2)}) collective-permute-start(bf16[1,16,4,512]{3,2,1,0:T(4,128)(2,1)S(1)} %reshape.97), channel_id=1, source_target_pairs={{36,0},{40,4},{44,8},{48,12},{52,16},{56,20},{60,24},{64,28},{68,3... | collective-permute-start | bytes 196616 | tf_op jit(solution)/shard_map/ppermute | solution.py:19
  139.8 11.6 %collective-permute-start.24 = (bf16[1,16,4,512]{3,2,1,0:T(4,128)(2,1)S(1)}, bf16[1,16,4,512]{3,2,1,0:T(4,128)(2,1)S(1)}, u32[]{:S(2)}, u32[]{:S(2)}) collective-permute-start(bf16[1,16,4,512]{3,2,1,0:T(4,128)(2,1)S(1)} %reshape.97), channel_id=1, source_target_pairs={{40,0},{44,4},{48,8},{52,12},{56,16},{60,20},{64,24},{68,28},{72,3... | collective-permute-start | bytes 196616 | tf_op jit(solution)/shard_map/ppermute | solution.py:19
  143.5 13.5 %collective-permute-start.25 = (bf16[1,16,4,512]{3,2,1,0:T(4,128)(2,1)S(1)}, bf16[1,16,4,512]{3,2,1,0:T(4,128)(2,1)S(1)}, u32[]{:S(2)}, u32[]{:S(2)}) collective-permute-start(bf16[1,16,4,512]{3,2,1,0:T(4,128)(2,1)S(1)} %reshape.97), channel_id=1, source_target_pairs={{44,0},{48,4},{52,8},{56,12},{60,16},{64,20},{68,24},{72,28},{76,3... | collective-permute-start | bytes 196616 | tf_op jit(solution)/shard_map/ppermute | solution.py:19
  144.8 14.9 %collective-permute-start.26 = (bf16[1,16,4,512]{3,2,1,0:T(4,128)(2,1)S(1)}, bf16[1,16,4,512]{3,2,1,0:T(4,128)(2,1)S(1)}, u32[]{:S(2)}, u32[]{:S(2)}) collective-permute-start(bf16[1,16,4,512]{3,2,1,0:T(4,128)(2,1)S(1)} %reshape.97), channel_id=1, source_target_pairs={{48,0},{52,4},{56,8},{60,12},{64,16},{68,20},{72,24},{76,28},{80,3... | collective-permute-start | bytes 196616 | tf_op jit(solution)/shard_map/ppermute | solution.py:19
  146.3 21.7 %collective-permute-start.27 = (bf16[1,16,4,512]{3,2,1,0:T(4,128)(2,1)S(1)}, bf16[1,16,4,512]{3,2,1,0:T(4,128)(2,1)S(1)}, u32[]{:S(2)}, u32[]{:S(2)}) collective-permute-start(bf16[1,16,4,512]{3,2,1,0:T(4,128)(2,1)S(1)} %reshape.97), channel_id=1, source_target_pairs={{52,0},{56,4},{60,8},{64,12},{68,16},{72,20},{76,24},{80,28},{84,3... | collective-permute-start | bytes 196616 | tf_op jit(solution)/shard_map/ppermute | solution.py:19
  148.7 19.8 %collective-permute-start.28 = (bf16[1,16,4,512]{3,2,1,0:T(4,128)(2,1)S(1)}, bf16[1,16,4,512]{3,2,1,0:T(4,128)(2,1)S(1)}, u32[]{:S(2)}, u32[]{:S(2)}) collective-permute-start(bf16[1,16,4,512]{3,2,1,0:T(4,128)(2,1)S(1)} %reshape.97), channel_id=1, source_target_pairs={{56,0},{60,4},{64,8},{68,12},{72,16},{76,20},{80,24},{84,28},{88,3... | collective-permute-start | bytes 196616 | tf_op jit(solution)/shard_map/ppermute | solution.py:19
  151.4 19.3 %collective-permute-start.29 = (bf16[1,16,4,512]{3,2,1,0:T(4,128)(2,1)S(1)}, bf16[1,16,4,512]{3,2,1,0:T(4,128)(2,1)S(1)}, u32[]{:S(2)}, u32[]{:S(2)}) collective-permute-start(bf16[1,16,4,512]{3,2,1,0:T(4,128)(2,1)S(1)} %reshape.97), channel_id=1, source_target_pairs={{60,0},{64,4},{68,8},{72,12},{76,16},{80,20},{84,24},{88,28},{92,3... | collective-permute-start | bytes 196616 | tf_op jit(solution)/shard_map/ppermute | solution.py:19
  186.8 1.6 copy-start
  188.4 1.6 copy-start.1
  188.4 2.2 copy-start.2
Sparse Core Ops, SparseCore 0:
  203.7 94.9 all-reduce.2
where the time goes:
time: 309 us; the launch traced here: 308 us
  waiting for transfers between devices  147 us (48%)
  starting transfers between devices  96.5 us (31%)
  matrix products  20.7 us (7%)
  local copies, waits for them, and re-layouts  20.3 us (7%)
  between operations  18.6 us (6%)
  other arithmetic  4.67 us (2%)
    unnamed x2, waiting for transfers between devices  93.2 us
    ppermute x30, starting transfers between devices, from_behind(): lax.ppermute(value, axis, [(source, source + steps) for source in range(i...  77.9 us
    ppermute x30, waiting for transfers between devices, from_behind(): lax.ppermute(value, axis, [(source, source + steps) for source in range(i...  27.9 us
    all_to_all x1, waiting for transfers between devices, local(): lax.all_to_all(raw, 'ch', split_axis=2, concat_axis=1, tiled=True)  25.9 us
    all_to_all x1, starting transfers between devices, local(): lax.all_to_all(raw, 'ch', split_axis=2, concat_axis=1, tiled=True)  18.5 us
    dot_general x3, matrix products, correlate(): jnp.dot(cross_spec.reshape(-1, 2 * half_len), inverse, preferred_element_...  10.2 us
    unnamed x42, local copies, waits for them, and re-layouts  8.24 us
    dynamic_slice x4, local copies, waits for them, and re-layouts, local(): sources = lax.dynamic_slice_in_dim(window[0], source_start, SRC, 0)  6.39 us
  transfers between devices with their start and end apart: 32, of which 14 were waited for; matrix products, arithmetic and copies ran while one was open for 1% of the time, Pallas kernels for 0%

commit v1 on v0

--- a/solution.py
+++ b/solution.py
@@ -81,7 +81,9 @@
 
 
 def local(raw, order, pair_blocks):
-    recorded = lax.all_to_all(raw, "ch", split_axis=2, concat_axis=1, tiled=True)
+    recorded = jnp.concatenate(
+        lax.all_to_all(jnp.stack(jnp.split(raw, lax.axis_size("ch"), axis=2)), "ch", 0, 0), axis=1
+    )
     local_channels = recorded.shape[2]
     onehot = (order[0][:, None] == jnp.arange(local_channels, dtype=jnp.int32)[None, :]).astype(
         jnp.bfloat16

time: 309 us -> 461 us (1.49)
  local copies, waits for them, and re-layouts: 20.3 us -> 186 us
  waiting for transfers between devices: 147 us -> 130 us
    unnamed x42 -> x164, local copies, waits for them, and re-layouts: 8.24 us -> 173 us
    all_to_all x1, waiting for transfers between devices: 25.9 us -> 8.93 us  [local(): lax.all_to_all(jnp.stack(jnp.split(raw, lax.axis_size('ch'), axis=2)), 'c...]
  transfers between devices with their start and end apart: 32 -> 32, of which waited for: 14 -> 12; matrix products, arithmetic and copies ran while one was open for 1% -> 1% of each run, Pallas kernels for 0% -> 0%
where the time goes in v1:
time: 461 us; the launch traced here: 457 us
  local copies, waits for them, and re-layouts  186 us (40%)
  waiting for transfers between devices  130 us (28%)
  starting transfers between devices  95.9 us (21%)
  matrix products  21.4 us (5%)
  between operations  18.6 us (4%)
  other arithmetic  4.68 us (1%)
    unnamed x164, local copies, waits for them, and re-layouts  173 us
    unnamed x2, waiting for transfers between devices  93.3 us
    ppermute x30, starting transfers between devices, from_behind(): lax.ppermute(value, axis, [(source, source + steps) for source in range(i...  77.5 us
    ppermute x30, waiting for transfers between devices, from_behind(): lax.ppermute(value, axis, [(source, source + steps) for source in range(i...  27.6 us
    all_to_all x1, starting transfers between devices, local(): lax.all_to_all(jnp.stack(jnp.split(raw, lax.axis_size('ch'), axis=2)), 'c...  18.4 us
    dot_general x3, matrix products, correlate(): jnp.dot(cross_spec.reshape(-1, 2 * half_len), inverse, preferred_element_...  10.2 us
  transfers between devices with their start and end apart: 32, of which 12 were waited for; matrix products, arithmetic and copies ran while one was open for 1% of the time, Pallas kernels for 0%

profile of v1, /device:TPU:1, one launch (start us, length us, event | category | flops | bytes accessed | tf_op | source)
XLA Modules:
  0.0 456.8 jit_solution(9434692322281128259)
XLA Ops:
  7.8 1.3 constant_dynamic-update-slice_fusion.126
  9.1 1.3 constant_dynamic-update-slice_fusion.125
  10.5 1.3 constant_dynamic-update-slice_fusion.124
  11.8 1.3 constant_dynamic-update-slice_fusion.123
  13.1 1.3 constant_dynamic-update-slice_fusion.122
  14.4 1.3 constant_dynamic-update-slice_fusion.121
  15.8 1.3 constant_dynamic-update-slice_fusion.120
  18.4 1.3 constant_dynamic-update-slice_fusion.118
  19.7 1.3 constant_dynamic-update-slice_fusion.117
  21.0 1.3 constant_dynamic-update-slice_fusion.116
  22.4 1.3 constant_dynamic-update-slice_fusion.115
  23.7 1.3 constant_dynamic-update-slice_fusion.114
  25.0 1.3 constant_dynamic-update-slice_fusion.113
  26.4 1.3 constant_dynamic-update-slice_fusion.112
  28.9 1.3 constant_dynamic-update-slice_fusion.110
  30.3 1.3 constant_dynamic-update-slice_fusion.109
  31.6 1.3 constant_dynamic-update-slice_fusion.108
  32.9 1.3 constant_dynamic-update-slice_fusion.107
  34.3 1.3 constant_dynamic-update-slice_fusion.106
  35.6 1.3 constant_dynamic-update-slice_fusion.105
  36.9 1.3 constant_dynamic-update-slice_fusion.104
  39.5 1.3 constant_dynamic-update-slice_fusion.102
  40.8 1.3 constant_dynamic-update-slice_fusion.101
  42.2 1.3 constant_dynamic-update-slice_fusion.100
  43.5 1.3 constant_dynamic-update-slice_fusion.99
  175.7 18.4 %all-to-all-start = ((bf16[128,1,8,16]{3,2,1,0:T(8,128)(2,1)}), bf16[128,1,8,16]{3,2,1,0:T(8,128)(2,1)S(1)}, u32[]{:S(2)}, u32[]{:S(2)}) async-start(bf16[128,1,8,16]{3,2,1,0:T(8,128)(2,1)} %constant_dynamic-update-slice_fusion), calls=%async_computation | async-start | bytes 524288 | tf_op jit(solution)/shard_map/all_to_all | solution.py:85
  194.2 1.4 fusion.98
  199.4 8.9 %all-to-all-done = bf16[128,1,8,16]{3,2,1,0:T(8,128)(2,1)S(1)} async-done(((bf16[128,1,8,16]{3,2,1,0:T(8,128)(2,1)}), bf16[128,1,8,16]{3,2,1,0:T(8,128)(2,1)S(1)}, u32[]{:S(2)}, u32[]{:S(2)}) %all-to-all-start) | async-done | bytes 32800 | tf_op jit(solution)/shard_map/all_to_all | solution.py:85
  209.3 2.4 fusion.47
  212.2 4.0 collective-permute-start
  216.2 1.6 collective-permute-start.1
  217.9 3.2 collective-permute-start.2
  221.0 4.7 %collective-permute-start.3 = (bf16[1,16,4,512]{3,2,1,0:T(4,128)(2,1)S(1)}, bf16[1,16,4,512]{3,2,1,0:T(4,128)(2,1)S(1)}, u32[]{:S(2)}, u32[]{:S(2)}) collective-permute-start(bf16[1,16,4,512]{3,2,1,0:T(4,128)(2,1)S(1)} %reshape.96), channel_id=1, source_target_pairs={{0,48},{4,52},{8,56},{12,60},{16,64},{20,68},{24,72},{28,76},{32,8... | collective-permute-start | bytes 196616 | tf_op jit(solution)/shard_map/ppermute | solution.py:19
  225.8 4.6 collective-permute-start.4
  231.2 3.2 collective-permute-start.5
  234.4 6.0 %collective-permute-start.6 = (bf16[1,16,4,512]{3,2,1,0:T(4,128)(2,1)S(1)}, bf16[1,16,4,512]{3,2,1,0:T(4,128)(2,1)S(1)}, u32[]{:S(2)}, u32[]{:S(2)}) collective-permute-start(bf16[1,16,4,512]{3,2,1,0:T(4,128)(2,1)S(1)} %reshape.96), channel_id=1, source_target_pairs={{0,36},{4,40},{8,44},{12,48},{16,52},{20,56},{24,60},{28,64},{32,6... | collective-permute-start | bytes 196616 | tf_op jit(solution)/shard_map/ppermute | solution.py:19
  240.4 3.9 collective-permute-start.7
  244.4 6.6 %collective-permute-start.8 = (bf16[1,16,4,512]{3,2,1,0:T(4,128)(2,1)S(1)}, bf16[1,16,4,512]{3,2,1,0:T(4,128)(2,1)S(1)}, u32[]{:S(2)}, u32[]{:S(2)}) collective-permute-start(bf16[1,16,4,512]{3,2,1,0:T(4,128)(2,1)S(1)} %reshape.96), channel_id=1, source_target_pairs={{0,28},{4,32},{8,36},{12,40},{16,44},{20,48},{24,52},{28,56},{32,6... | collective-permute-start | bytes 196616 | tf_op jit(solution)/shard_map/ppermute | solution.py:19
  251.1 1.8 collective-permute-start.9
  252.9 5.4 %collective-permute-start.10 = (bf16[1,16,4,512]{3,2,1,0:T(4,128)(2,1)S(1)}, bf16[1,16,4,512]{3,2,1,0:T(4,128)(2,1)S(1)}, u32[]{:S(2)}, u32[]{:S(2)}) collective-permute-start(bf16[1,16,4,512]{3,2,1,0:T(4,128)(2,1)S(1)} %reshape.96), channel_id=1, source_target_pairs={{0,20},{4,24},{8,28},{12,32},{16,36},{20,40},{24,44},{28,48},{32,5... | collective-permute-start | bytes 196616 | tf_op jit(solution)/shard_map/ppermute | solution.py:19
  258.3 3.9 collective-permute-start.11
  262.3 4.1 collective-permute-start.12
  266.5 1.6 collective-permute-start.13
  268.1 2.8 collective-permute-start.14
  271.0 1.9 collective-permute-start.15
  281.1 1.5 collective-permute-done.17
  285.9 3.8 collective-permute-done.19
  291.0 2.7 collective-permute-done.20
  300.0 1.5 collective-permute-start.29
  301.5 5.2 %collective-permute-done.25 = bf16[1,16,4,512]{3,2,1,0:T(4,128)(2,1)S(1)} collective-permute-done((bf16[1,16,4,512]{3,2,1,0:T(4,128)(2,1)S(1)}, bf16[1,16,4,512]{3,2,1,0:T(4,128)(2,1)S(1)}, u32[]{:S(2)}, u32[]{:S(2)}) %collective-permute-start.25) | collective-permute-done | bytes 65568 | tf_op jit(solution)/shard_map/ppermute | solution.py:19
  306.8 2.3 collective-permute-done.26
  309.1 8.1 %collective-permute-done.27 = bf16[1,16,4,512]{3,2,1,0:T(4,128)(2,1)S(1)} collective-permute-done((bf16[1,16,4,512]{3,2,1,0:T(4,128)(2,1)S(1)}, bf16[1,16,4,512]{3,2,1,0:T(4,128)(2,1)S(1)}, u32[]{:S(2)}, u32[]{:S(2)}) %collective-permute-start.27) | collective-permute-done | bytes 65568 | tf_op jit(solution)/shard_map/ppermute | solution.py:19
  317.7 2.0 collective-permute-done.29
  319.7 1.5 constant_dynamic-slice_fusion.2
  322.5 2.0 convolution_bitcast_fusion.4
  324.5 2.1 copy.418
  327.9 2.0 convolution_bitcast_fusion.3
  329.8 1.9 convolution_bitcast_fusion.2
  331.8 2.2 copy.422
  339.9 3.4 fusion.15
  343.3 3.4 fusion.18
  347.1 3.4 fusion.21
  350.5 2.0 pad_maximum_fusion
  354.5 93.3 %all-reduce.3.cloned.1.call-done = bf16[16,3,128,256]{3,2,0,1:T(8,128)(2,1)} async-done(((bf16[16,3,128,256]{3,2,0,1:T(8,128)(2,1)}), bf16[16,3,128,256]{3,2,0,1:T(8,128)(2,1)}) %all-reduce.3.cloned.1.call-update) | async-done | bytes 3145744
  (206 shorter events, 170.5 us)
Async XLA Ops:
  175.7 32.6 %all-to-all-start = ((bf16[128,1,8,16]{3,2,1,0:T(8,128)(2,1)}), bf16[128,1,8,16]{3,2,1,0:T(8,128)(2,1)S(1)}, u32[]{:S(2)}, u32[]{:S(2)}) async-start(bf16[128,1,8,16]{3,2,1,0:T(8,128)(2,1)} %constant_dynamic-update-slice_fusion), calls=%async_computation | async-start | bytes 524288 | tf_op jit(solution)/shard_map/all_to_all | solution.py:85
  194.1 253.6 %all-reduce.3.cloned.1.call-start = ((), (), s32[]{:S(2)}) async-start(), calls=%async_computation.1 | async-start | bytes 6291456
  212.2 19.0 %collective-permute-start = (bf16[1,16,4,512]{3,2,1,0:T(4,128)(2,1)S(1)}, bf16[1,16,4,512]{3,2,1,0:T(4,128)(2,1)S(1)}, u32[]{:S(2)}, u32[]{:S(2)}) collective-permute-start(bf16[1,16,4,512]{3,2,1,0:T(4,128)(2,1)S(1)} %reshape.96), channel_id=1, source_target_pairs={{0,60},{4,64},{8,68},{12,72},{16,76},{20,80},{24,84},{28,88},{32,9... | collective-permute-start | bytes 196616 | tf_op jit(solution)/shard_map/ppermute | solution.py:19
  216.2 18.2 %collective-permute-start.1 = (bf16[1,16,4,512]{3,2,1,0:T(4,128)(2,1)S(1)}, bf16[1,16,4,512]{3,2,1,0:T(4,128)(2,1)S(1)}, u32[]{:S(2)}, u32[]{:S(2)}) collective-permute-start(bf16[1,16,4,512]{3,2,1,0:T(4,128)(2,1)S(1)} %reshape.96), channel_id=1, source_target_pairs={{0,56},{4,60},{8,64},{12,68},{16,72},{20,76},{24,80},{28,84},{32,8... | collective-permute-start | bytes 196616 | tf_op jit(solution)/shard_map/ppermute | solution.py:19
  217.9 22.6 %collective-permute-start.2 = (bf16[1,16,4,512]{3,2,1,0:T(4,128)(2,1)S(1)}, bf16[1,16,4,512]{3,2,1,0:T(4,128)(2,1)S(1)}, u32[]{:S(2)}, u32[]{:S(2)}) collective-permute-start(bf16[1,16,4,512]{3,2,1,0:T(4,128)(2,1)S(1)} %reshape.96), channel_id=1, source_target_pairs={{0,52},{4,56},{8,60},{12,64},{16,68},{20,72},{24,76},{28,80},{32,8... | collective-permute-start | bytes 196616 | tf_op jit(solution)/shard_map/ppermute | solution.py:19
  221.0 23.3 %collective-permute-start.3 = (bf16[1,16,4,512]{3,2,1,0:T(4,128)(2,1)S(1)}, bf16[1,16,4,512]{3,2,1,0:T(4,128)(2,1)S(1)}, u32[]{:S(2)}, u32[]{:S(2)}) collective-permute-start(bf16[1,16,4,512]{3,2,1,0:T(4,128)(2,1)S(1)} %reshape.96), channel_id=1, source_target_pairs={{0,48},{4,52},{8,56},{12,60},{16,64},{20,68},{24,72},{28,76},{32,8... | collective-permute-start | bytes 196616 | tf_op jit(solution)/shard_map/ppermute | solution.py:19
  225.8 25.3 %collective-permute-start.4 = (bf16[1,16,4,512]{3,2,1,0:T(4,128)(2,1)S(1)}, bf16[1,16,4,512]{3,2,1,0:T(4,128)(2,1)S(1)}, u32[]{:S(2)}, u32[]{:S(2)}) collective-permute-start(bf16[1,16,4,512]{3,2,1,0:T(4,128)(2,1)S(1)} %reshape.96), channel_id=1, source_target_pairs={{0,44},{4,48},{8,52},{12,56},{16,60},{20,64},{24,68},{28,72},{32,7... | collective-permute-start | bytes 196616 | tf_op jit(solution)/shard_map/ppermute | solution.py:19
  231.2 21.7 %collective-permute-start.5 = (bf16[1,16,4,512]{3,2,1,0:T(4,128)(2,1)S(1)}, bf16[1,16,4,512]{3,2,1,0:T(4,128)(2,1)S(1)}, u32[]{:S(2)}, u32[]{:S(2)}) collective-permute-start(bf16[1,16,4,512]{3,2,1,0:T(4,128)(2,1)S(1)} %reshape.96), channel_id=1, source_target_pairs={{0,40},{4,44},{8,48},{12,52},{16,56},{20,60},{24,64},{28,68},{32,7... | collective-permute-start | bytes 196616 | tf_op jit(solution)/shard_map/ppermute | solution.py:19
  234.4 23.9 %collective-permute-start.6 = (bf16[1,16,4,512]{3,2,1,0:T(4,128)(2,1)S(1)}, bf16[1,16,4,512]{3,2,1,0:T(4,128)(2,1)S(1)}, u32[]{:S(2)}, u32[]{:S(2)}) collective-permute-start(bf16[1,16,4,512]{3,2,1,0:T(4,128)(2,1)S(1)} %reshape.96), channel_id=1, source_target_pairs={{0,36},{4,40},{8,44},{12,48},{16,52},{20,56},{24,60},{28,64},{32,6... | collective-permute-start | bytes 196616 | tf_op jit(solution)/shard_map/ppermute | solution.py:19
  240.4 21.8 %collective-permute-start.7 = (bf16[1,16,4,512]{3,2,1,0:T(4,128)(2,1)S(1)}, bf16[1,16,4,512]{3,2,1,0:T(4,128)(2,1)S(1)}, u32[]{:S(2)}, u32[]{:S(2)}) collective-permute-start(bf16[1,16,4,512]{3,2,1,0:T(4,128)(2,1)S(1)} %reshape.96), channel_id=1, source_target_pairs={{0,32},{4,36},{8,40},{12,44},{16,48},{20,52},{24,56},{28,60},{32,6... | collective-permute-start | bytes 196616 | tf_op jit(solution)/shard_map/ppermute | solution.py:19
  244.4 22.1 %collective-permute-start.8 = (bf16[1,16,4,512]{3,2,1,0:T(4,128)(2,1)S(1)}, bf16[1,16,4,512]{3,2,1,0:T(4,128)(2,1)S(1)}, u32[]{:S(2)}, u32[]{:S(2)}) collective-permute-start(bf16[1,16,4,512]{3,2,1,0:T(4,128)(2,1)S(1)} %reshape.96), channel_id=1, source_target_pairs={{0,28},{4,32},{8,36},{12,40},{16,44},{20,48},{24,52},{28,56},{32,6... | collective-permute-start | bytes 196616 | tf_op jit(solution)/shard_map/ppermute | solution.py:19
  251.1 17.1 %collective-permute-start.9 = (bf16[1,16,4,512]{3,2,1,0:T(4,128)(2,1)S(1)}, bf16[1,16,4,512]{3,2,1,0:T(4,128)(2,1)S(1)}, u32[]{:S(2)}, u32[]{:S(2)}) collective-permute-start(bf16[1,16,4,512]{3,2,1,0:T(4,128)(2,1)S(1)} %reshape.96), channel_id=1, source_target_pairs={{0,24},{4,28},{8,32},{12,36},{16,40},{20,44},{24,48},{28,52},{32,5... | collective-permute-start | bytes 196616 | tf_op jit(solution)/shard_map/ppermute | solution.py:19
  252.9 18.1 %collective-permute-start.10 = (bf16[1,16,4,512]{3,2,1,0:T(4,128)(2,1)S(1)}, bf16[1,16,4,512]{3,2,1,0:T(4,128)(2,1)S(1)}, u32[]{:S(2)}, u32[]{:S(2)}) collective-permute-start(bf16[1,16,4,512]{3,2,1,0:T(4,128)(2,1)S(1)} %reshape.96), channel_id=1, source_target_pairs={{0,20},{4,24},{8,28},{12,32},{16,36},{20,40},{24,44},{28,48},{32,5... | collective-permute-start | bytes 196616 | tf_op jit(solution)/shard_map/ppermute | solution.py:19
  258.3 14.6 %collective-permute-start.11 = (bf16[1,16,4,512]{3,2,1,0:T(4,128)(2,1)S(1)}, bf16[1,16,4,512]{3,2,1,0:T(4,128)(2,1)S(1)}, u32[]{:S(2)}, u32[]{:S(2)}) collective-permute-start(bf16[1,16,4,512]{3,2,1,0:T(4,128)(2,1)S(1)} %reshape.96), channel_id=1, source_target_pairs={{0,16},{4,20},{8,24},{12,28},{16,32},{20,36},{24,40},{28,44},{32,4... | collective-permute-start | bytes 196616 | tf_op jit(solution)/shard_map/ppermute | solution.py:19
  262.3 12.0 %collective-permute-start.12 = (bf16[1,16,4,512]{3,2,1,0:T(4,128)(2,1)S(1)}, bf16[1,16,4,512]{3,2,1,0:T(4,128)(2,1)S(1)}, u32[]{:S(2)}, u32[]{:S(2)}) collective-permute-start(bf16[1,16,4,512]{3,2,1,0:T(4,128)(2,1)S(1)} %reshape.96), channel_id=1, source_target_pairs={{0,12},{4,16},{8,20},{12,24},{16,28},{20,32},{24,36},{28,40},{32,4... | collective-permute-start | bytes 196616 | tf_op jit(solution)/shard_map/ppermute | solution.py:19
  266.5 9.2 %collective-permute-start.13 = (bf16[1,16,4,512]{3,2,1,0:T(4,128)(2,1)S(1)}, bf16[1,16,4,512]{3,2,1,0:T(4,128)(2,1)S(1)}, u32[]{:S(2)}, u32[]{:S(2)}) collective-permute-start(bf16[1,16,4,512]{3,2,1,0:T(4,128)(2,1)S(1)} %reshape.96), channel_id=1, source_target_pairs={{0,8},{4,12},{8,16},{12,20},{16,24},{20,28},{24,32},{28,36},{32,40... | collective-permute-start | bytes 196616 | tf_op jit(solution)/shard_map/ppermute | solution.py:19
  268.1 8.8 %collective-permute-start.14 = (bf16[1,16,4,512]{3,2,1,0:T(4,128)(2,1)S(1)}, bf16[1,16,4,512]{3,2,1,0:T(4,128)(2,1)S(1)}, u32[]{:S(2)}, u32[]{:S(2)}) collective-permute-start(bf16[1,16,4,512]{3,2,1,0:T(4,128)(2,1)S(1)} %reshape.96), channel_id=1, source_target_pairs={{0,4},{4,8},{8,12},{12,16},{16,20},{20,24},{24,28},{28,32},{32,36}... | collective-permute-start | bytes 196616 | tf_op jit(solution)/shard_map/ppermute | solution.py:19
  271.0 7.4 %collective-permute-start.15 = (bf16[1,16,4,512]{3,2,1,0:T(4,128)(2,1)S(1)}, bf16[1,16,4,512]{3,2,1,0:T(4,128)(2,1)S(1)}, u32[]{:S(2)}, u32[]{:S(2)}) collective-permute-start(bf16[1,16,4,512]{3,2,1,0:T(4,128)(2,1)S(1)} %reshape.96), channel_id=1, source_target_pairs={{4,0},{8,4},{12,8},{16,12},{20,16},{24,20},{28,24},{32,28},{36,32}... | collective-permute-start | bytes 196616 | tf_op jit(solution)/shard_map/ppermute | solution.py:19
  272.9 6.8 %collective-permute-start.16 = (bf16[1,16,4,512]{3,2,1,0:T(4,128)(2,1)S(1)}, bf16[1,16,4,512]{3,2,1,0:T(4,128)(2,1)S(1)}, u32[]{:S(2)}, u32[]{:S(2)}) collective-permute-start(bf16[1,16,4,512]{3,2,1,0:T(4,128)(2,1)S(1)} %reshape.96), channel_id=1, source_target_pairs={{8,0},{12,4},{16,8},{20,12},{24,16},{28,20},{32,24},{36,28},{40,32... | collective-permute-start | bytes 196616 | tf_op jit(solution)/shard_map/ppermute | solution.py:19
  274.3 8.3 %collective-permute-start.17 = (bf16[1,16,4,512]{3,2,1,0:T(4,128)(2,1)S(1)}, bf16[1,16,4,512]{3,2,1,0:T(4,128)(2,1)S(1)}, u32[]{:S(2)}, u32[]{:S(2)}) collective-permute-start(bf16[1,16,4,512]{3,2,1,0:T(4,128)(2,1)S(1)} %reshape.96), channel_id=1, source_target_pairs={{12,0},{16,4},{20,8},{24,12},{28,16},{32,20},{36,24},{40,28},{44,3... | collective-permute-start | bytes 196616 | tf_op jit(solution)/shard_map/ppermute | solution.py:19
  275.6 8.9 %collective-permute-start.18 = (bf16[1,16,4,512]{3,2,1,0:T(4,128)(2,1)S(1)}, bf16[1,16,4,512]{3,2,1,0:T(4,128)(2,1)S(1)}, u32[]{:S(2)}, u32[]{:S(2)}) collective-permute-start(bf16[1,16,4,512]{3,2,1,0:T(4,128)(2,1)S(1)} %reshape.96), channel_id=1, source_target_pairs={{16,0},{20,4},{24,8},{28,12},{32,16},{36,20},{40,24},{44,28},{48,3... | collective-permute-start | bytes 196616 | tf_op jit(solution)/shard_map/ppermute | solution.py:19
  277.0 12.7 %collective-permute-start.19 = (bf16[1,16,4,512]{3,2,1,0:T(4,128)(2,1)S(1)}, bf16[1,16,4,512]{3,2,1,0:T(4,128)(2,1)S(1)}, u32[]{:S(2)}, u32[]{:S(2)}) collective-permute-start(bf16[1,16,4,512]{3,2,1,0:T(4,128)(2,1)S(1)} %reshape.96), channel_id=1, source_target_pairs={{20,0},{24,4},{28,8},{32,12},{36,16},{40,20},{44,24},{48,28},{52,3... | collective-permute-start | bytes 196616 | tf_op jit(solution)/shard_map/ppermute | solution.py:19
  278.4 15.3 %collective-permute-start.20 = (bf16[1,16,4,512]{3,2,1,0:T(4,128)(2,1)S(1)}, bf16[1,16,4,512]{3,2,1,0:T(4,128)(2,1)S(1)}, u32[]{:S(2)}, u32[]{:S(2)}) collective-permute-start(bf16[1,16,4,512]{3,2,1,0:T(4,128)(2,1)S(1)} %reshape.96), channel_id=1, source_target_pairs={{24,0},{28,4},{32,8},{36,12},{40,16},{44,20},{48,24},{52,28},{56,3... | collective-permute-start | bytes 196616 | tf_op jit(solution)/shard_map/ppermute | solution.py:19
  279.7 15.2 %collective-permute-start.21 = (bf16[1,16,4,512]{3,2,1,0:T(4,128)(2,1)S(1)}, bf16[1,16,4,512]{3,2,1,0:T(4,128)(2,1)S(1)}, u32[]{:S(2)}, u32[]{:S(2)}) collective-permute-start(bf16[1,16,4,512]{3,2,1,0:T(4,128)(2,1)S(1)} %reshape.96), channel_id=1, source_target_pairs={{28,0},{32,4},{36,8},{40,12},{44,16},{48,20},{52,24},{56,28},{60,3... | collective-permute-start | bytes 196616 | tf_op jit(solution)/shard_map/ppermute | solution.py:19
  282.5 13.8 %collective-permute-start.22 = (bf16[1,16,4,512]{3,2,1,0:T(4,128)(2,1)S(1)}, bf16[1,16,4,512]{3,2,1,0:T(4,128)(2,1)S(1)}, u32[]{:S(2)}, u32[]{:S(2)}) collective-permute-start(bf16[1,16,4,512]{3,2,1,0:T(4,128)(2,1)S(1)} %reshape.96), channel_id=1, source_target_pairs={{32,0},{36,4},{40,8},{44,12},{48,16},{52,20},{56,24},{60,28},{64,3... | collective-permute-start | bytes 196616 | tf_op jit(solution)/shard_map/ppermute | solution.py:19
  284.6 13.1 %collective-permute-start.23 = (bf16[1,16,4,512]{3,2,1,0:T(4,128)(2,1)S(1)}, bf16[1,16,4,512]{3,2,1,0:T(4,128)(2,1)S(1)}, u32[]{:S(2)}, u32[]{:S(2)}) collective-permute-start(bf16[1,16,4,512]{3,2,1,0:T(4,128)(2,1)S(1)} %reshape.96), channel_id=1, source_target_pairs={{36,0},{40,4},{44,8},{48,12},{52,16},{56,20},{60,24},{64,28},{68,3... | collective-permute-start | bytes 196616 | tf_op jit(solution)/shard_map/ppermute | solution.py:19
  289.6 10.4 %collective-permute-start.24 = (bf16[1,16,4,512]{3,2,1,0:T(4,128)(2,1)S(1)}, bf16[1,16,4,512]{3,2,1,0:T(4,128)(2,1)S(1)}, u32[]{:S(2)}, u32[]{:S(2)}) collective-permute-start(bf16[1,16,4,512]{3,2,1,0:T(4,128)(2,1)S(1)} %reshape.96), channel_id=1, source_target_pairs={{40,0},{44,4},{48,8},{52,12},{56,16},{60,20},{64,24},{68,28},{72,3... | collective-permute-start | bytes 196616 | tf_op jit(solution)/shard_map/ppermute | solution.py:19
  293.6 13.1 %collective-permute-start.25 = (bf16[1,16,4,512]{3,2,1,0:T(4,128)(2,1)S(1)}, bf16[1,16,4,512]{3,2,1,0:T(4,128)(2,1)S(1)}, u32[]{:S(2)}, u32[]{:S(2)}) collective-permute-start(bf16[1,16,4,512]{3,2,1,0:T(4,128)(2,1)S(1)} %reshape.96), channel_id=1, source_target_pairs={{44,0},{48,4},{52,8},{56,12},{60,16},{64,20},{68,24},{72,28},{76,3... | collective-permute-start | bytes 196616 | tf_op jit(solution)/shard_map/ppermute | solution.py:19
  295.0 14.1 %collective-permute-start.26 = (bf16[1,16,4,512]{3,2,1,0:T(4,128)(2,1)S(1)}, bf16[1,16,4,512]{3,2,1,0:T(4,128)(2,1)S(1)}, u32[]{:S(2)}, u32[]{:S(2)}) collective-permute-start(bf16[1,16,4,512]{3,2,1,0:T(4,128)(2,1)S(1)} %reshape.96), channel_id=1, source_target_pairs={{48,0},{52,4},{56,8},{60,12},{64,16},{68,20},{72,24},{76,28},{80,3... | collective-permute-start | bytes 196616 | tf_op jit(solution)/shard_map/ppermute | solution.py:19
  296.3 20.8 %collective-permute-start.27 = (bf16[1,16,4,512]{3,2,1,0:T(4,128)(2,1)S(1)}, bf16[1,16,4,512]{3,2,1,0:T(4,128)(2,1)S(1)}, u32[]{:S(2)}, u32[]{:S(2)}) collective-permute-start(bf16[1,16,4,512]{3,2,1,0:T(4,128)(2,1)S(1)} %reshape.96), channel_id=1, source_target_pairs={{52,0},{56,4},{60,8},{64,12},{68,16},{72,20},{76,24},{80,28},{84,3... | collective-permute-start | bytes 196616 | tf_op jit(solution)/shard_map/ppermute | solution.py:19
  297.7 20.0 %collective-permute-start.28 = (bf16[1,16,4,512]{3,2,1,0:T(4,128)(2,1)S(1)}, bf16[1,16,4,512]{3,2,1,0:T(4,128)(2,1)S(1)}, u32[]{:S(2)}, u32[]{:S(2)}) collective-permute-start(bf16[1,16,4,512]{3,2,1,0:T(4,128)(2,1)S(1)} %reshape.96), channel_id=1, source_target_pairs={{56,0},{60,4},{64,8},{68,12},{72,16},{76,20},{80,24},{84,28},{88,3... | collective-permute-start | bytes 196616 | tf_op jit(solution)/shard_map/ppermute | solution.py:19
  300.0 19.6 %collective-permute-start.29 = (bf16[1,16,4,512]{3,2,1,0:T(4,128)(2,1)S(1)}, bf16[1,16,4,512]{3,2,1,0:T(4,128)(2,1)S(1)}, u32[]{:S(2)}, u32[]{:S(2)}) collective-permute-start(bf16[1,16,4,512]{3,2,1,0:T(4,128)(2,1)S(1)} %reshape.96), channel_id=1, source_target_pairs={{60,0},{64,4},{68,8},{72,12},{76,16},{80,20},{84,24},{88,28},{92,3... | collective-permute-start | bytes 196616 | tf_op jit(solution)/shard_map/ppermute | solution.py:19
  335.7 1.6 copy-start
  337.3 1.6 copy-start.1
  337.3 2.2 copy-start.2
Sparse Core Ops, SparseCore 0:
  352.6 95.0 all-reduce.2
